TPU v7x, 32 devices: a whole 2x2x4 slice. The times are simulated.
32 devices in a mesh: row: 4 (over y, x), col: 8 (over z, core).
Axes of the slice: x: 2, y: 2, z: 4, core: 2. Of those that a mesh axis runs over, the one named last changes fastest.
Arguments:
- slab: bfloat16 [1024, 16384], P(('row', 'col')), may hold values from -0.1875 to 0.1875
- block_mask: int32 [32, 16], P(('row', 'col')), may hold values 0 or 1
- damping: float32 [16384], replicated, may hold values from 0.05 to 2
Outputs:
- hessian: float32 [16384, 16384], P('row', 'col')
All inputs are finite; a program needn't handle non-finite values. No bound on the sum of `block_mask` on one device may be relied on, other than what follows from the above.
Results may differ from a plain program's by a relative error of at most 0.0003.
Values may be sent and summed in bfloat16 or wider, within the bound.
No kernel may reach another device: no remote copies, remote signals or barrier semaphores. Data moves between devices by JAX's collectives and lax.ppermute only.
A program may use at most 128 MiB of HBM per device.

v0:
```python
import jax
import jax.numpy as jnp
from jax import lax
from jax.sharding import PartitionSpec as P


def shards(slab, block_mask, damping):
    local_rows = slab.shape[0]
    width = slab.shape[1]
    row_count = lax.axis_size("row")
    col_count = lax.axis_size("col")
    row_width = width // row_count
    col_width = width // col_count
    block_count = block_mask.shape[1]
    column_mask = jnp.repeat(block_mask[0], width // block_count).astype(jnp.bfloat16)
    masked = slab * column_mask[None, :]
    row_parts = masked.reshape(local_rows, row_count, row_width)
    row_parts = lax.all_to_all(row_parts, "row", split_axis=1, concat_axis=0, tiled=True)
    row_parts = row_parts.reshape(row_count * local_rows, row_width)
    row_panel = lax.all_gather(row_parts, "col", axis=0, tiled=True)
    row_panel = row_panel.reshape(col_count, row_count, local_rows, row_width)
    row_panel = jnp.transpose(row_panel, (1, 0, 2, 3)).reshape(
        row_count * col_count * local_rows, row_width
    )
    col_parts = masked.reshape(local_rows, col_count, col_width)
    col_parts = lax.all_to_all(col_parts, "col", split_axis=1, concat_axis=0, tiled=True)
    col_parts = col_parts.reshape(col_count * local_rows, col_width)
    block = lax.dot_general(
        row_panel,
        lax.all_gather(col_parts, "row", axis=0, tiled=True),
        (((0,), (0,)), ((), ())),
        preferred_element_type=jnp.float32,
    )
    row_start = lax.axis_index("row") * row_width
    col_start = lax.axis_index("col") * col_width
    global_rows = row_start + jnp.arange(row_width, dtype=jnp.int32)
    global_cols = col_start + jnp.arange(col_width, dtype=jnp.int32)
    row_damping = lax.dynamic_slice_in_dim(damping, row_start, row_width, 0)
    on_diagonal = global_rows[:, None] == global_cols[None, :]
    return block + jnp.where(on_diagonal, row_damping[:, None], jnp.float32(0.0))


def solution(mesh):
    placed = (P(("row", "col"), None), P(("row", "col"), None), P())
    return jax.shard_map(
        shards, mesh=mesh, in_specs=placed, out_specs=P("row", "col"), check_vma=False
    )
```

profile of v0, /device:TPU:0, one launch (start us, length us, event | category | flops | bytes accessed | tf_op | source)
XLA Modules:
  0.0 214.2 jit_solution(16617587774653621209)
XLA Ops:
  6.5 0.0 all-gather.3.cloned.1.call-start
  6.5 0.7 convert_bitcast_fusion
  7.2 0.1 broadcast_bitcast_fusion
  7.3 1.4 broadcast_multiply_fusion
  8.6 0.1 copy.17
  8.7 19.2 %all_to_all.30 = bf16[32,4,4096]{2,0,1:T(8,128)(2,1)} all-to-all(bf16[32,4,4096]{2,0,1:T(8,128)(2,1)S(1)} %bitcast.36), channel_id=1, replica_groups=mesh['row'=4,'col'=8] {'row'}, dimensions={1} | all-to-all | bytes 2097152 | tf_op jit(solution)/shard_map/all_to_all | solution.py:18
  27.9 0.0 all-gather.3.cloned.1.call-update
  28.0 0.0 all-gather.5.cloned.1.call-start
  28.0 0.1 copy.16
  28.1 54.8 %all_to_all.31 = bf16[32,8,2048]{2,0,1:T(8,128)(2,1)} all-to-all(bf16[32,8,2048]{2,0,1:T(8,128)(2,1)S(1)} %bitcast.35), channel_id=1, replica_groups=mesh['row'=4,'col'=8] {'col'}, dimensions={1} | all-to-all | bytes 2097152 | tf_op jit(solution)/shard_map/all_to_all | solution.py:26
  82.9 0.0 all-gather.5.cloned.1.call-update
  82.9 45.7 %all-gather.3.cloned.1.call-done = bf16[1024,4096]{1,0:T(8,128)(2,1)} async-done(((bf16[128,4096]{1,0:T(8,128)(2,1)}), bf16[1024,4096]{1,0:T(8,128)(2,1)}) %all-gather.3.cloned.1.call-update) | async-done | bytes 8388624 | tf_op jit(solution)/shard_map/all_gather | solution.py:20
  128.7 0.0 dynamic-slice-start
  128.7 8.2 %copy.9 = bf16[8,4,32,4096]{3,2,0,1:T(8,128)(2,1)} copy(bf16[8,4,32,4096]{3,2,1,0:T(8,128)(2,1)} %bitcast.31) | data formatting | bytes 16777216 | tf_op jit(solution)/shard_map/reshape | solution.py:21
  136.9 43.8 %all-gather.5.cloned.1.call-done = bf16[1024,2048]{1,0:T(8,128)(2,1)} async-done(((bf16[256,2048]{1,0:T(8,128)(2,1)}), bf16[1024,2048]{1,0:T(8,128)(2,1)}) %all-gather.5.cloned.1.call-update) | async-done | bytes 4194320 | tf_op jit(solution)/shard_map/all_gather | solution.py:30
  180.7 0.0 dynamic-slice-done
  180.7 26.7 %select_add_fusion = f32[4096,2048]{1,0:T(8,128)} fusion(bf16[1024,4096]{1,0:T(8,128)(2,1)} %bitcast.32, bf16[1024,2048]{1,0:T(8,128)(2,1)} %all-gather.5.cloned.1.call-done, f32[4096]{0:T(1024)S(1)} %dynamic-slice-done, s32[2048]{0:T(1024)S(1)} %iota_add_fusion.1, s32[4096]{0:T(1024)S(1)} %iota_add_fusion), kind=kOutput, calls=%fused_computation | convolution fusion | flops 17205035008 | bytes 46178304 | tf_op jit(solution)/shard_map/dot_general | solution.py:28
  (3 shorter events, 0.0 us)
Async XLA Ops:
  6.5 122.1 %all-gather.3.cloned.1.call-start = ((), (), s32[]{:S(2)}) async-start(), calls=%async_computation.2 | async-start | bytes 9437184 | tf_op jit(solution)/shard_map/all_gather | solution.py:20
  28.0 152.7 %all-gather.5.cloned.1.call-start = ((), (), s32[]{:S(2)}) async-start(), calls=%async_computation.3 | async-start | bytes 5242880 | tf_op jit(solution)/shard_map/all_gather | solution.py:30
  128.7 52.0 %dynamic-slice-start = ((f32[16384]{0:T(1024)}, s32[]{:T(128)}), f32[4096]{0:T(1024)S(1)}, s32[]{:S(2)}) async-start(f32[16384]{0:T(1024)} %param.5, s32[]{:T(128)} %select_n.7), calls=%async_computation.4 | async-start | bytes 33280 | tf_op jit(solution)/shard_map/dynamic_slice | solution.py:38
Sparse Core Ops, SparseCore 0:
  28.1 100.5 all-gather.2
  130.5 50.1 all-gather.4
where the time goes:
time: 214 us
  waiting for transfers between devices  89.5 us (42%)
  blocking collectives  74 us (35%)
  matrix products  26.7 us (12%)
  between operations  13.4 us (6%)
  local copies, waits for them, and re-layouts  8.49 us (4%)
    all_to_all x1, blocking collectives, shards(): lax.all_to_all(col_parts, 'col', split_axis=1, concat_axis=0, tiled=True)  54.8 us
    all_gather x1, waiting for transfers between devices, shards(): row_panel = lax.all_gather(row_parts, 'col', axis=0, tiled=True)  45.7 us
    all_gather x1, waiting for transfers between devices, shards(): lax.all_gather(col_parts, 'row', axis=0, tiled=True)  43.8 us
    dot_general x1, matrix products, shards(): lax.dot_general(row_panel, lax.all_gather(col_parts, 'row', axis=0, tiled...  26.7 us
    all_to_all x1, blocking collectives, shards(): lax.all_to_all(row_parts, 'row', split_axis=1, concat_axis=0, tiled=True)  19.2 us
    reshape x1, local copies, waits for them, and re-layouts, shards(): row_panel = row_panel.reshape(col_count, row_count, local_rows, row_width)  8.21 us
  transfers between devices with their start and end apart: 2, of which 2 were waited for; matrix products, arithmetic and copies ran while one was open for 4% of the time, Pallas kernels for 0%

commit v1 on v0

--- a/solution.py
+++ b/solution.py
@@ -1,7 +1,31 @@
+import functools
 import jax
 import jax.numpy as jnp
 from jax import lax
 from jax.sharding import PartitionSpec as P
+
+
+def edit_meshes(work_x, peer_axis):
+    x_now, t1 = (jax.lax.axis_size(peer_axis), jax.lax.axis_index(peer_axis))
+    now = list(work_x.shape)
+    wide_out = work_x.shape[1] // x_now
+    now[1] = wide_out
+    v_next = now[0]
+    now[0] = v_next * x_now
+    block_last = jnp.zeros(now, work_x.dtype)
+    for src_i in tuple(range(x_now)):
+        arr_out = lax.dynamic_slice_in_dim(work_x, (t1 ^ src_i) * wide_out, wide_out, axis=1)
+        if src_i:
+            arr_out = jax.lax.ppermute(
+                arr_out, axis_name=peer_axis, perm=[(b, b ^ src_i) for b in range(x_now)]
+            )
+        block_last = lax.dynamic_update_slice_in_dim(
+            block_last, arr_out, (t1 ^ src_i) * v_next, axis=0
+        )
+    return block_last
+
+
+find_the_spans = functools.partial(edit_meshes, peer_axis="col")
 
 
 def shards(slab, block_mask, damping):
@@ -23,7 +47,7 @@
         row_count * col_count * local_rows, row_width
     )
     col_parts = masked.reshape(local_rows, col_count, col_width)
-    col_parts = lax.all_to_all(col_parts, "col", split_axis=1, concat_axis=0, tiled=True)
+    col_parts = find_the_spans(col_parts)
     col_parts = col_parts.reshape(col_count * local_rows, col_width)
     block = lax.dot_general(
         row_panel,

time: 214 us -> 236 us (1.10)
  waiting for transfers between devices: 89.5 us -> 145 us
  blocking collectives: 74 us -> 19.2 us
  starting transfers between devices: 0.04 us -> 14.6 us
  local copies, waits for them, and re-layouts: 8.49 us -> 14.7 us
    ppermute x0 -> x7, waiting for transfers between devices: none -> 88.4 us  [edit_meshes(): jax.lax.ppermute(arr_out, axis_name=peer_axis, perm=[(b, b ^ src_i) for b...]
    all_to_all x1 -> x0, blocking collectives: 54.8 us -> none  [shards(): lax.all_to_all(col_parts, 'col', split_axis=1, concat_axis=0, tiled=True)]
    all_gather x1, waiting for transfers between devices: 45.7 us -> 12.4 us  [shards(): row_panel = lax.all_gather(row_parts, 'col', axis=0, tiled=True)]
    ppermute x0 -> x7, starting transfers between devices: none -> 14.6 us  [edit_meshes(): jax.lax.ppermute(arr_out, axis_name=peer_axis, perm=[(b, b ^ src_i) for b...]
    dynamic_slice x0 -> x1, local copies, waits for them, and re-layouts: none -> 3.13 us  [edit_meshes(): lax.dynamic_slice_in_dim(work_x, (t1 ^ src_i) * wide_out, wide_out, axis=1)]
  transfers between devices with their start and end apart: 2 -> 9, of which waited for: 2 -> 6; matrix products, arithmetic and copies ran while one was open for 4% -> 6% of each run, Pallas kernels for 0% -> 0%
where the time goes in v1:
time: 236 us
  waiting for transfers between devices  145 us (61%)
  matrix products  26.7 us (11%)
  blocking collectives  19.2 us (8%)
  local copies, waits for them, and re-layouts  14.7 us (6%)
  starting transfers between devices  14.6 us (6%)
  between operations  13.7 us (6%)
    ppermute x7, waiting for transfers between devices, edit_meshes(): jax.lax.ppermute(arr_out, axis_name=peer_axis, perm=[(b, b ^ src_i) for b...  88.4 us
    all_gather x1, waiting for transfers between devices, shards(): lax.all_gather(col_parts, 'row', axis=0, tiled=True)  44.1 us
    dot_general x1, matrix products, shards(): lax.dot_general(row_panel, lax.all_gather(col_parts, 'row', axis=0, tiled...  26.7 us
    all_to_all x1, blocking collectives, shards(): lax.all_to_all(row_parts, 'row', split_axis=1, concat_axis=0, tiled=True)  19.2 us
    ppermute x7, starting transfers between devices, edit_meshes(): jax.lax.ppermute(arr_out, axis_name=peer_axis, perm=[(b, b ^ src_i) for b...  14.6 us
    all_gather x1, waiting for transfers between devices, shards(): row_panel = lax.all_gather(row_parts, 'col', axis=0, tiled=True)  12.4 us
    reshape x1, local copies, waits for them, and re-layouts, shards(): row_panel = row_panel.reshape(col_count, row_count, local_rows, row_width)  8.09 us
  transfers between devices with their start and end apart: 9, of which 6 were waited for; matrix products, arithmetic and copies ran while one was open for 6% of the time, Pallas kernels for 0%

profile of v1, /device:TPU:0, one launch (start us, length us, event | category | flops | bytes accessed | tf_op | source)
XLA Modules:
  0.0 235.8 jit_solution(3824276108405293901)
XLA Ops:
  6.5 0.0 all-gather.3.cloned.1.call-start
  6.5 0.7 convert_bitcast_fusion
  7.2 0.1 broadcast_bitcast_fusion
  7.3 1.4 broadcast_multiply_fusion
  8.6 0.1 copy.29
  8.7 19.2 %all_to_all.15 = bf16[32,4,4096]{2,0,1:T(8,128)(2,1)} all-to-all(bf16[32,4,4096]{2,0,1:T(8,128)(2,1)S(1)} %bitcast.44), channel_id=1, replica_groups=mesh['row'=4,'col'=8] {'row'}, dimensions={1} | all-to-all | bytes 2097152 | tf_op jit(solution)/shard_map/all_to_all | solution.py:42
  27.9 0.0 all-gather.3.cloned.1.call-update
  28.0 0.0 all-gather.5.cloned.1.call-start
  28.1 0.6 copy.19
  28.7 3.1 %constant_dynamic-slice_fusion = (bf16[32,1,2048]{2,1,0:T(2,128)(2,1)S(1)}, bf16[32,1,2048]{2,1,0:T(2,128)(2,1)S(1)}, bf16[32,1,2048]{2,1,0:T(2,128)(2,1)S(1)}, ...) fusion(bf16[32,8,2048]{2,1,0:T(8,128)(2,1)S(1)} %bitcast.38, ...), kind=kLoop, calls=%fused_computation.14 | loop fusion | bytes 2097184 | tf_op jit(solution)/shard_map/dynamic_slice | solution.py:17
  31.8 1.5 collective-permute-start.6
  33.3 2.1 collective-permute-start.5
  35.5 0.4 collective-permute-start.4
  35.9 2.2 collective-permute-start.3
  38.1 0.2 collective-permute-start
  38.2 0.1 reshape.72
  38.3 0.1 bitcast_dynamic-update-slice_fusion.7
  38.5 1.4 collective-permute-done
  39.9 1.3 collective-permute-start.1
  41.3 1.0 bitcast_dynamic-update-slice_fusion.6
  42.3 43.1 %collective-permute-done.1 = bf16[32,1,2048]{2,1,0:T(2,128)(2,1)S(1)} collective-permute-done((bf16[32,1,2048]{2,1,0:T(2,128)(2,1)}, bf16[32,1,2048]{2,1,0:T(2,128)(2,1)S(1)}, u32[]{:S(2)}, u32[]{:S(2)}) %collective-permute-start.1) | collective-permute-done | bytes 131104 | tf_op jit(solution)/shard_map/ppermute | solution.py:19
  85.4 6.8 %collective-permute-start.2 = (bf16[32,1,2048]{2,1,0:T(2,128)(2,1)}, bf16[32,1,2048]{2,1,0:T(2,128)(2,1)S(1)}, u32[]{:S(2)}, u32[]{:S(2)}) collective-permute-start(bf16[32,1,2048]{2,1,0:T(2,128)(2,1)} %get-tuple-element.9), channel_id=1, source_target_pairs={{0,3},{1,2},{2,1},{3,0},{4,7},{5,6},{6,5},{7,4},{8,11},{9,10},{10,... | collective-permute-start | bytes 393224 | tf_op jit(solution)/shard_map/ppermute | solution.py:19
  92.3 0.1 bitcast_dynamic-update-slice_fusion.5
  92.3 25.6 %collective-permute-done.2 = bf16[32,1,2048]{2,1,0:T(2,128)(2,1)S(1)} collective-permute-done((bf16[32,1,2048]{2,1,0:T(2,128)(2,1)}, bf16[32,1,2048]{2,1,0:T(2,128)(2,1)S(1)}, u32[]{:S(2)}, u32[]{:S(2)}) %collective-permute-start.2) | collective-permute-done | bytes 131104 | tf_op jit(solution)/shard_map/ppermute | solution.py:19
  118.0 0.1 bitcast_dynamic-update-slice_fusion.4
  118.1 18.1 %collective-permute-done.3 = bf16[32,1,2048]{2,1,0:T(2,128)(2,1)S(1)} collective-permute-done((bf16[32,1,2048]{2,1,0:T(2,128)(2,1)S(1)}, bf16[32,1,2048]{2,1,0:T(2,128)(2,1)S(1)}, u32[]{:S(2)}, u32[]{:S(2)}) %collective-permute-start.3) | collective-permute-done | bytes 131104 | tf_op jit(solution)/shard_map/ppermute | solution.py:19
  136.2 0.1 bitcast_dynamic-update-slice_fusion.3
  136.3 0.0 collective-permute-done.4
  136.3 0.1 bitcast_dynamic-update-slice_fusion.2
  136.4 0.0 collective-permute-done.5
  136.4 0.1 bitcast_dynamic-update-slice_fusion.1
  136.5 0.0 collective-permute-done.6
  136.5 0.1 bitcast_dynamic-update-slice_fusion
  136.6 0.0 copy-start
  136.6 1.0 copy-done
  137.6 0.0 all-gather.5.cloned.1.call-update
  137.6 12.4 %all-gather.3.cloned.1.call-done = bf16[1024,4096]{1,0:T(8,128)(2,1)} async-done(((bf16[128,4096]{1,0:T(8,128)(2,1)}), bf16[1024,4096]{1,0:T(8,128)(2,1)}) %all-gather.3.cloned.1.call-update) | async-done | bytes 8388624 | tf_op jit(solution)/shard_map/all_gather | solution.py:44
  150.0 0.0 dynamic-slice-start
  150.0 8.1 %copy.8 = bf16[8,4,32,4096]{3,2,0,1:T(8,128)(2,1)} copy(bf16[8,4,32,4096]{3,2,1,0:T(8,128)(2,1)} %bitcast.41) | data formatting | bytes 16777216 | tf_op jit(solution)/shard_map/reshape | solution.py:45
  158.1 44.1 %all-gather.5.cloned.1.call-done = bf16[1024,2048]{1,0:T(8,128)(2,1)} async-done(((bf16[256,2048]{1,0:T(8,128)(2,1)}), bf16[1024,2048]{1,0:T(8,128)(2,1)}) %all-gather.5.cloned.1.call-update) | async-done | bytes 4194320 | tf_op jit(solution)/shard_map/all_gather | solution.py:54
  202.2 0.0 dynamic-slice-done
  202.2 26.7 %select_add_fusion = f32[4096,2048]{1,0:T(8,128)} fusion(bf16[1024,4096]{1,0:T(8,128)(2,1)} %bitcast.42, bf16[1024,2048]{1,0:T(8,128)(2,1)} %all-gather.5.cloned.1.call-done, f32[4096]{0:T(1024)S(1)} %dynamic-slice-done, s32[2048]{0:T(1024)S(1)} %iota_add_fusion.1, s32[4096]{0:T(1024)S(1)} %iota_add_fusion), kind=kOutput, calls=%fused_computation | convolution fusion | flops 17205035008 | bytes 46178304 | tf_op jit(solution)/shard_map/dot_general | solution.py:52
  (3 shorter events, 0.0 us)
Async XLA Ops:
  6.5 143.5 %all-gather.3.cloned.1.call-start = ((), (), s32[]{:S(2)}) async-start(), calls=%async_computation.1 | async-start | bytes 9437184 | tf_op jit(solution)/shard_map/all_gather | solution.py:44
  28.0 174.2 %all-gather.5.cloned.1.call-start = ((), (), s32[]{:S(2)}) async-start(), calls=%async_computation.2 | async-start | bytes 5242880 | tf_op jit(solution)/shard_map/all_gather | solution.py:54
  31.8 104.7 %collective-permute-start.6 = (bf16[32,1,2048]{2,1,0:T(2,128)(2,1)S(1)}, bf16[32,1,2048]{2,1,0:T(2,128)(2,1)S(1)}, u32[]{:S(2)}, u32[]{:S(2)}) collective-permute-start(bf16[32,1,2048]{2,1,0:T(2,128)(2,1)S(1)} %get-tuple-element.5), channel_id=1, source_target_pairs={{0,7},{1,6},{2,5},{3,4},{4,3},{5,2},{6,1},{7,0},{8,15},{9,14},{10,... | collective-permute-start | bytes 393224 | tf_op jit(solution)/shard_map/ppermute | solution.py:19
  33.3 103.1 %collective-permute-start.5 = (bf16[32,1,2048]{2,1,0:T(2,128)(2,1)S(1)}, bf16[32,1,2048]{2,1,0:T(2,128)(2,1)S(1)}, u32[]{:S(2)}, u32[]{:S(2)}) collective-permute-start(bf16[32,1,2048]{2,1,0:T(2,128)(2,1)S(1)} %get-tuple-element.6), channel_id=1, source_target_pairs={{0,6},{1,7},{2,4},{3,5},{4,2},{5,3},{6,0},{7,1},{8,14},{9,15},{10,... | collective-permute-start | bytes 393224 | tf_op jit(solution)/shard_map/ppermute | solution.py:19
  35.5 100.9 %collective-permute-start.4 = (bf16[32,1,2048]{2,1,0:T(2,128)(2,1)S(1)}, bf16[32,1,2048]{2,1,0:T(2,128)(2,1)S(1)}, u32[]{:S(2)}, u32[]{:S(2)}) collective-permute-start(bf16[32,1,2048]{2,1,0:T(2,128)(2,1)S(1)} %get-tuple-element.7), channel_id=1, source_target_pairs={{0,5},{1,4},{2,7},{3,6},{4,1},{5,0},{6,3},{7,2},{8,13},{9,12},{10,... | collective-permute-start | bytes 393224 | tf_op jit(solution)/shard_map/ppermute | solution.py:19
  35.9 100.3 %collective-permute-start.3 = (bf16[32,1,2048]{2,1,0:T(2,128)(2,1)S(1)}, bf16[32,1,2048]{2,1,0:T(2,128)(2,1)S(1)}, u32[]{:S(2)}, u32[]{:S(2)}) collective-permute-start(bf16[32,1,2048]{2,1,0:T(2,128)(2,1)S(1)} %get-tuple-element.8), channel_id=1, source_target_pairs={{0,4},{1,5},{2,6},{3,7},{4,0},{5,1},{6,2},{7,3},{8,12},{9,13},{10,... | collective-permute-start | bytes 393224 | tf_op jit(solution)/shard_map/ppermute | solution.py:19
  38.1 1.9 collective-permute-start
  39.9 45.5 %collective-permute-start.1 = (bf16[32,1,2048]{2,1,0:T(2,128)(2,1)}, bf16[32,1,2048]{2,1,0:T(2,128)(2,1)S(1)}, u32[]{:S(2)}, u32[]{:S(2)}) collective-permute-start(bf16[32,1,2048]{2,1,0:T(2,128)(2,1)} %get-tuple-element.10), channel_id=1, source_target_pairs={{0,2},{1,3},{2,0},{3,1},{4,6},{5,7},{6,4},{7,5},{8,10},{9,11},{10,... | collective-permute-start | bytes 393224 | tf_op jit(solution)/shard_map/ppermute | solution.py:19
  85.4 32.6 %collective-permute-start.2 = (bf16[32,1,2048]{2,1,0:T(2,128)(2,1)}, bf16[32,1,2048]{2,1,0:T(2,128)(2,1)S(1)}, u32[]{:S(2)}, u32[]{:S(2)}) collective-permute-start(bf16[32,1,2048]{2,1,0:T(2,128)(2,1)} %get-tuple-element.9), channel_id=1, source_target_pairs={{0,3},{1,2},{2,1},{3,0},{4,7},{5,6},{6,5},{7,4},{8,11},{9,10},{10,... | collective-permute-start | bytes 393224 | tf_op jit(solution)/shard_map/ppermute | solution.py:19
  136.6 1.0 copy-start
  150.0 52.2 %dynamic-slice-start = ((f32[16384]{0:T(1024)}, s32[]{:T(128)}), f32[4096]{0:T(1024)S(1)}, s32[]{:S(2)}) async-start(f32[16384]{0:T(1024)} %param.5, s32[]{:T(128)} %select_n.71), calls=%async_computation.3 | async-start | bytes 33280 | tf_op jit(solution)/shard_map/dynamic_slice | solution.py:62
Sparse Core Ops, SparseCore 0:
  28.1 121.8 all-gather.2
  151.9 50.2 all-gather.4
